TPU v7x, 32 devices: a whole 2x2x4 slice. The times are simulated.
32 devices in a mesh: row: 8 (over y, x, core), col: 4 (over z).
Axes of the slice: x: 2, y: 2, z: 4, core: 2. Of those that a mesh axis runs over, the one named last changes fastest.
Arguments:
- inverse_tiles: float32 [512, 512], P('row', 'col'), may hold values from -0.375 to 0.375
- factor_panels: float32 [3, 512, 256], P(None, 'row', 'col'), may hold values from -6 to 6
- block_rows: int32 [3, 8], replicated, may hold values from 0 to 15, as said below
- couplings: float32 [2, 512, 512], replicated, may hold values from -0.25 to 0.25
Outputs:
- new_columns: float32 [3, 512, 512], P(None, ('row', 'col'))
Inputs may be any that keep to these rules, and one draw needn't show every extreme that they name: `block_rows`: each row lists 8 different row blocks in no particular order; in each row, all 4 blocks q * 4 to q * 4 + 3 of some q are listed.
All inputs are finite; a program needn't handle non-finite values.
Results may differ from a plain program's by a relative error of at most 0.0001.
Values sent between devices are 32-bit elements; how exact they have to be, the bound alone decides.
No kernel may reach another device: no remote copies, remote signals or barrier semaphores. Data moves between devices by JAX's collectives and lax.ppermute only.
A program may use at most 64 MiB of HBM per device.

v0:
```python
import jax
import jax.numpy as jnp
from jax import lax
from jax.sharding import PartitionSpec as P


def on_device(inverse_tiles, factor_panels, block_rows, couplings):
    tile_rows, tile_cols = inverse_tiles.shape
    piece_rows = factor_panels.shape[1]
    listed = block_rows.shape[1]
    col_count = lax.axis_size("col")
    block_size = factor_panels.shape[2] * col_count // listed
    local_blocks = tile_cols // block_size
    my_column = lax.axis_index("col")
    offset = my_column * local_blocks
    targets = offset + jnp.arange(local_blocks, dtype=jnp.int32)
    results = []
    previous = None
    for section in range(factor_panels.shape[0]):
        section_rows = block_rows[section]
        gathered = lax.all_gather(factor_panels[section], "col", axis=1, tiled=True)
        onehot = (section_rows[:, None] == targets[None, :]).astype(jnp.float32)
        picked = jnp.einsum(
            "wpr,pq->wqr",
            gathered.reshape(piece_rows, listed, block_size),
            onehot,
            precision=lax.Precision.HIGHEST,
        ).reshape(piece_rows, tile_cols)
        partial_value = lax.dot_general(
            inverse_tiles,
            lax.all_gather(picked, "row", axis=0, tiled=True),
            (((1,), (1,)), ((), ())),
            precision=lax.Precision.HIGHEST,
            preferred_element_type=jnp.float32,
        )
        summed = lax.psum_scatter(partial_value, "col", scatter_dimension=0, tiled=True)
        if previous is not None:
            summed = summed + jnp.dot(
                previous,
                couplings[section - 1],
                precision=lax.Precision.HIGHEST,
                preferred_element_type=jnp.float32,
            )
        previous = -summed
        results.append(previous)
    return jnp.stack(results)


def solution(mesh):
    return jax.shard_map(
        on_device,
        mesh=mesh,
        in_specs=(P("row", "col"), P(None, "row", "col"), P(), P()),
        out_specs=P(None, ("row", "col"), None),
        check_vma=False,
    )
```

profile of v0, /device:TPU:0, one launch (start us, length us, event | category | flops | bytes accessed | tf_op | source)
XLA Modules:
  0.0 111.6 jit_solution(15987718816973304762)
XLA Ops:
  6.5 0.8 fusion.23
  7.3 0.1 copy.26
  7.4 15.1 %all-gather = f32[1,64,256]{1,2,0:T(8,128)S(1)} all-gather(f32[1,64,64]{1,2,0:T(8,128)S(1)} %copy.26), channel_id=2, replica_groups=mesh['row'=8,'col'=4] {'col'}, dimensions={2}, use_global_device_ids=true | all-gather | bytes 81920 | tf_op jit(solution)/shard_map/all_gather | solution.py:21
  22.5 0.8 slice_bitcast_fusion.2
  23.3 0.3 convolution_bitcast_fusion.5
  23.6 0.1 copy.17
  23.7 9.4 %all_gather.19 = f32[512,128]{1,0:T(8,128)S(1)} all-gather(f32[64,128]{1,0:T(8,128)S(1)} %copy.17), channel_id=1, replica_groups=mesh['row'=8,'col'=4] {'row'}, dimensions={0}, use_global_device_ids=true | all-gather | bytes 294912 | tf_op jit(solution)/shard_map/all_gather | solution.py:31
  33.1 1.1 convolution_bitcast_fusion.2
  34.3 0.1 copy.27
  34.3 13.5 %all-gather.1 = f32[1,64,256]{1,2,0:T(8,128)S(1)} all-gather(f32[1,64,64]{1,2,0:T(8,128)S(1)} %copy.27), channel_id=3, replica_groups=mesh['row'=8,'col'=4] {'col'}, dimensions={2}, use_global_device_ids=true | all-gather | bytes 81920 | tf_op jit(solution)/shard_map/all_gather | solution.py:21
  47.9 0.3 convolution_bitcast_fusion.4
  48.2 0.1 copy.21
  48.2 9.3 %all_gather.21 = f32[512,128]{1,0:T(8,128)S(1)} all-gather(f32[64,128]{1,0:T(8,128)S(1)} %copy.21), channel_id=1, replica_groups=mesh['row'=8,'col'=4] {'row'}, dimensions={0}, use_global_device_ids=true | all-gather | bytes 294912 | tf_op jit(solution)/shard_map/all_gather | solution.py:31
  57.5 1.1 convolution_bitcast_fusion.1
  58.6 0.1 copy.28
  58.7 13.7 %all-gather.2 = f32[1,64,256]{1,2,0:T(8,128)S(1)} all-gather(f32[1,64,64]{1,2,0:T(8,128)S(1)} %copy.28), channel_id=4, replica_groups=mesh['row'=8,'col'=4] {'col'}, dimensions={2}, use_global_device_ids=true | all-gather | bytes 81920 | tf_op jit(solution)/shard_map/all_gather | solution.py:21
  72.4 0.3 convolution_bitcast_fusion.3
  72.8 8.7 %all_gather.23 = f32[512,128]{1,0:T(8,128)S(1)} all-gather(f32[64,128]{1,0:T(8,128)S(1)} %copy.25), channel_id=1, replica_groups=mesh['row'=8,'col'=4] {'row'}, dimensions={0}, use_global_device_ids=true | all-gather | bytes 294912 | tf_op jit(solution)/shard_map/all_gather | solution.py:31
  81.5 1.1 convolution_bitcast_fusion
  82.7 0.8 negate_bitcast_fusion
  83.4 1.4 %fusion.2 = f32[16,512]{1,0:T(8,128)S(1)} fusion(f32[16,512]{1,0:T(8,128)} %reduce-scatter.6.cloned.1.call-done, f32[2,512,512]{2,1,0:T(8,128)S(1)} %copy-done.1, f32[16,512]{1,0:T(8,128)} %reduce-scatter.4.cloned.1.call-done), kind=kOutput, calls=%fused_computation.10 | convolution fusion | flops 50356224 | bytes 1146880 | tf_op jit(solution)/shard_map/dot_general | solution.py:38
  84.8 18.2 %reduce-scatter.8.cloned.1.call-done = f32[16,512]{1,0:T(8,128)} async-done(((f32[64,512]{1,0:T(8,128)}), f32[16,512]{1,0:T(8,128)}) %reduce-scatter.8.cloned.1.call-update) | async-done | bytes 32784 | tf_op jit(solution)/shard_map/reduce_scatter | solution.py:36
  103.0 1.4 %fusion.1 = f32[1,16,512]{2,1,0:T(8,128)S(1)} fusion(f32[16,512]{1,0:T(8,128)} %reduce-scatter.8.cloned.1.call-done, f32[16,512]{1,0:T(8,128)S(1)} %fusion.2, f32[2,512,512]{2,1,0:T(8,128)S(1)} %copy-done.1), kind=kOutput, calls=%fused_computation.8 | convolution fusion | flops 50348032 | bytes 1146880 | tf_op jit(solution)/shard_map/dot_general | solution.py:38
  104.4 0.6 pad_maximum_fusion
  (17 shorter events, 0.3 us)
Async XLA Ops:
  6.5 26.6 %copy-start = (f32[64,128]{1,0:T(8,128)S(1)}, f32[64,128]{1,0:T(8,128)}, u32[]{:S(2)}) copy-start(f32[64,128]{1,0:T(8,128)} %param.4) | copy-start | bytes 98308
  6.5 76.1 %reduce-scatter.4.cloned.1.call-start = ((), (), s32[]{:S(2)}) async-start(), calls=%async_computation.3 | async-start | bytes 163840 | tf_op jit(solution)/shard_map/reduce_scatter | solution.py:36
  23.6 59.9 %copy-start.1 = (f32[2,512,512]{2,1,0:T(8,128)S(1)}, f32[2,512,512]{2,1,0:T(8,128)}, u32[]{:S(2)}) copy-start(f32[2,512,512]{2,1,0:T(8,128)} %param.7) | copy-start | bytes 6291460
  34.2 49.2 %reduce-scatter.6.cloned.1.call-start = ((), (), s32[]{:S(2)}) async-start(), calls=%async_computation.4 | async-start | bytes 163840 | tf_op jit(solution)/shard_map/reduce_scatter | solution.py:36
  58.6 44.4 %reduce-scatter.8.cloned.1.call-start = ((), (), s32[]{:S(2)}) async-start(), calls=%async_computation.5 | async-start | bytes 163840 | tf_op jit(solution)/shard_map/reduce_scatter | solution.py:36
Sparse Core Ops, SparseCore 0:
  34.3 19.9 reduce-scatter.3
  58.7 20.2 reduce-scatter.5
  82.8 20.2 reduce-scatter.7
where the time goes:
time: 112 us
  blocking collectives  69.8 us (62%)
  waiting for transfers between devices  18.3 us (16%)
  between operations  13.2 us (12%)
  matrix products  6.76 us (6%)
  local copies, waits for them, and re-layouts  2.04 us (2%)
  other arithmetic  1.41 us (1%)
    all_gather x3, blocking collectives, on_device(): gathered = lax.all_gather(factor_panels[section], 'col', axis=1, tiled=True)  42.3 us
    all_gather x3, blocking collectives, on_device(): lax.all_gather(picked, 'row', axis=0, tiled=True)  27.5 us
    reduce_scatter x3, waiting for transfers between devices, on_device(): lax.psum_scatter(partial_value, 'col', scatter_dimension=0, tiled=True)  18.2 us
    dot_general x3, matrix products, on_device(): lax.dot_general(inverse_tiles, lax.all_gather(picked, 'row', axis=0, tile...  3.21 us
    dot_general x2, matrix products, on_device(): jnp.dot(previous, couplings[section - 1], precision=lax.Precision.HIGHEST...  2.76 us
  transfers between devices with their start and end apart: 3, of which 1 were waited for; matrix products, arithmetic and copies ran while one was open for 5% of the time, Pallas kernels for 0%

commit v1 on v0

--- a/solution.py
+++ b/solution.py
@@ -2,6 +2,17 @@
 import jax.numpy as jnp
 from jax import lax
 from jax.sharding import PartitionSpec as P
+
+
+def turned_line(value, name, d):
+    count = lax.axis_size(name)
+    route = [(i, (i + 1) % count) for i in range(count)]
+    parts = [value]
+    for stride in range(1, count):
+        parts = [lax.ppermute(parts[0], name, route), *parts]
+    out = jnp.concatenate(parts, axis=d)
+    offset = (lax.axis_index(name) + 1) * parts[-1].shape[d]
+    return jnp.roll(out, offset, axis=d)
 
 
 def on_device(inverse_tiles, factor_panels, block_rows, couplings):
@@ -18,7 +29,7 @@
     previous = None
     for section in range(factor_panels.shape[0]):
         section_rows = block_rows[section]
-        gathered = lax.all_gather(factor_panels[section], "col", axis=1, tiled=True)
+        gathered = turned_line(factor_panels[section], "col", 1)
         onehot = (section_rows[:, None] == targets[None, :]).astype(jnp.float32)
         picked = jnp.einsum(
             "wpr,pq->wqr",

time: 112 us -> 104 us (0.929)
  blocking collectives: 69.8 us -> 27.5 us
  waiting for transfers between devices: 18.3 us -> 45.1 us
  starting transfers between devices: 0.09 us -> 6.95 us
    all_gather x3 -> x0, blocking collectives: 42.3 us -> none  [on_device(): gathered = lax.all_gather(factor_panels[section], 'col', axis=1, tiled=True)]
    reduce_scatter x3, waiting for transfers between devices: 18.2 us -> 34.3 us  [on_device(): lax.psum_scatter(partial_value, 'col', scatter_dimension=0, tiled=True)]
    ppermute x0 -> x9, waiting for transfers between devices: none -> 10.8 us  [turned_line(): parts = [lax.ppermute(parts[0], name, route), *parts]]
    ppermute x0 -> x9, starting transfers between devices: none -> 6.87 us  [turned_line(): parts = [lax.ppermute(parts[0], name, route), *parts]]
  transfers between devices with their start and end apart: 3 -> 12, of which waited for: 1 -> 9; matrix products, arithmetic and copies ran while one was open for 5% -> 8% of each run, Pallas kernels for 0% -> 0%
where the time goes in v1:
time: 104 us
  waiting for transfers between devices  45.1 us (43%)
  blocking collectives  27.5 us (26%)
  between operations  13.2 us (13%)
  starting transfers between devices  6.95 us (7%)
  matrix products  6.81 us (7%)
  other arithmetic  2.08 us (2%)
  local copies, waits for them, and re-layouts  2.04 us (2%)
    reduce_scatter x3, waiting for transfers between devices, on_device(): lax.psum_scatter(partial_value, 'col', scatter_dimension=0, tiled=True)  34.3 us
    all_gather x3, blocking collectives, on_device(): lax.all_gather(picked, 'row', axis=0, tiled=True)  27.5 us
    ppermute x9, waiting for transfers between devices, turned_line(): parts = [lax.ppermute(parts[0], name, route), *parts]  10.8 us
    ppermute x9, starting transfers between devices, turned_line(): parts = [lax.ppermute(parts[0], name, route), *parts]  6.87 us
    dot_general x3, matrix products, on_device(): lax.dot_general(inverse_tiles, lax.all_gather(picked, 'row', axis=0, tile...  3.23 us
    dot_general x2, matrix products, on_device(): jnp.dot(previous, couplings[section - 1], precision=lax.Precision.HIGHEST...  2.76 us
  transfers between devices with their start and end apart: 12, of which 9 were waited for; matrix products, arithmetic and copies ran while one was open for 8% of the time, Pallas kernels for 0%

profile of v1, /device:TPU:0, one launch (start us, length us, event | category | flops | bytes accessed | tf_op | source)
XLA Modules:
  0.0 103.7 jit_solution(17755596409267579146)
XLA Ops:
  6.5 0.8 fusion.44
  7.4 3.1 %collective-permute-start = (f32[64,64]{0,1:T(8,128)S(1)}, f32[64,64]{0,1:T(8,128)S(1)}, u32[]{:S(2)}, u32[]{:S(2)}) collective-permute-start(f32[64,64]{0,1:T(8,128)S(1)} %bitcast.65), channel_id=1, source_target_pairs={{0,1},{1,2},{2,3},{3,0},{4,5},{5,6},{6,7},{7,4},{8,9},{9,10},{10,1... | collective-permute-start | bytes 49160 | tf_op jit(solution)/shard_map/ppermute | solution.py:12
  10.6 1.6 %collective-permute-start.3 = (f32[64,64]{0,1:T(8,128)S(1)}, f32[64,64]{0,1:T(8,128)S(1)}, u32[]{:S(2)}, u32[]{:S(2)}) collective-permute-start(f32[64,64]{0,1:T(8,128)S(1)} %bitcast.61), channel_id=1, source_target_pairs={{0,1},{1,2},{2,3},{3,0},{4,5},{5,6},{6,7},{7,4},{8,9},{9,10},{10,1... | collective-permute-start | bytes 49160 | tf_op jit(solution)/shard_map/ppermute | solution.py:12
  12.2 1.6 %collective-permute-start.6 = (f32[64,64]{0,1:T(8,128)S(1)}, f32[64,64]{0,1:T(8,128)S(1)}, u32[]{:S(2)}, u32[]{:S(2)}) collective-permute-start(f32[64,64]{0,1:T(8,128)S(1)} %bitcast.63), channel_id=1, source_target_pairs={{0,1},{1,2},{2,3},{3,0},{4,5},{5,6},{6,7},{7,4},{8,9},{9,10},{10,1... | collective-permute-start | bytes 49160 | tf_op jit(solution)/shard_map/ppermute | solution.py:12
  13.9 0.6 collective-permute-done
  14.5 0.8 slice_bitcast_fusion.2
  15.3 1.3 %collective-permute-done.3 = f32[64,64]{0,1:T(8,128)S(1)} collective-permute-done((f32[64,64]{0,1:T(8,128)S(1)}, f32[64,64]{0,1:T(8,128)S(1)}, u32[]{:S(2)}, u32[]{:S(2)}) %collective-permute-start.3) | collective-permute-done | bytes 16416 | tf_op jit(solution)/shard_map/ppermute | solution.py:12
  16.9 1.3 %collective-permute-done.6 = f32[64,64]{0,1:T(8,128)S(1)} collective-permute-done((f32[64,64]{0,1:T(8,128)S(1)}, f32[64,64]{0,1:T(8,128)S(1)}, u32[]{:S(2)}, u32[]{:S(2)}) %collective-permute-start.6) | collective-permute-done | bytes 16416 | tf_op jit(solution)/shard_map/ppermute | solution.py:12
  18.4 1.7 %collective-permute-done.1 = f32[64,64]{0,1:T(8,128)S(1)} collective-permute-done((f32[64,64]{0,1:T(8,128)S(1)}, f32[64,64]{0,1:T(8,128)S(1)}, u32[]{:S(2)}, u32[]{:S(2)}) %collective-permute-start.1) | collective-permute-done | bytes 16416 | tf_op jit(solution)/shard_map/ppermute | solution.py:12
  20.2 2.2 %collective-permute-done.4 = f32[64,64]{0,1:T(8,128)S(1)} collective-permute-done((f32[64,64]{0,1:T(8,128)S(1)}, f32[64,64]{0,1:T(8,128)S(1)}, u32[]{:S(2)}, u32[]{:S(2)}) %collective-permute-start.4) | collective-permute-done | bytes 16416 | tf_op jit(solution)/shard_map/ppermute | solution.py:12
  22.4 1.8 %collective-permute-done.7 = f32[64,64]{0,1:T(8,128)S(1)} collective-permute-done((f32[64,64]{0,1:T(8,128)S(1)}, f32[64,64]{0,1:T(8,128)S(1)}, u32[]{:S(2)}, u32[]{:S(2)}) %collective-permute-start.7) | collective-permute-done | bytes 16416 | tf_op jit(solution)/shard_map/ppermute | solution.py:12
  24.1 1.8 %collective-permute-done.2 = f32[64,64]{0,1:T(8,128)S(1)} collective-permute-done((f32[64,64]{0,1:T(8,128)S(1)}, f32[64,64]{0,1:T(8,128)S(1)}, u32[]{:S(2)}, u32[]{:S(2)}) %collective-permute-start.2) | collective-permute-done | bytes 16416 | tf_op jit(solution)/shard_map/ppermute | solution.py:12
  26.7 9.8 %all_gather.9 = f32[512,128]{1,0:T(8,128)S(1)} all-gather(f32[64,128]{1,0:T(8,128)S(1)} %copy.17), channel_id=1, replica_groups=mesh['row'=8,'col'=4] {'row'}, dimensions={0}, use_global_device_ids=true | all-gather | bytes 294912 | tf_op jit(solution)/shard_map/all_gather | solution.py:42
  36.5 1.1 %convolution_bitcast_fusion.2 = f32[64,512]{1,0:T(8,128)} fusion(f32[512,128]{1,0:T(8,128)S(1)} %all_gather.9, f32[64,128]{1,0:T(8,128)S(1)} %copy-done), kind=kOutput, calls=%fused_computation.2 | convolution fusion | flops 50331648 | bytes 425984 | tf_op jit(solution)/shard_map/dot_general | solution.py:40
  38.7 9.3 %all_gather.10 = f32[512,128]{1,0:T(8,128)S(1)} all-gather(f32[64,128]{1,0:T(8,128)S(1)} %copy.21), channel_id=1, replica_groups=mesh['row'=8,'col'=4] {'row'}, dimensions={0}, use_global_device_ids=true | all-gather | bytes 294912 | tf_op jit(solution)/shard_map/all_gather | solution.py:42
  48.0 1.1 %convolution_bitcast_fusion.1 = f32[64,512]{1,0:T(8,128)} fusion(f32[512,128]{1,0:T(8,128)S(1)} %all_gather.10, f32[64,128]{1,0:T(8,128)S(1)} %copy-done), kind=kOutput, calls=%fused_computation.1 | convolution fusion | flops 50331648 | bytes 425984 | tf_op jit(solution)/shard_map/dot_general | solution.py:40
  49.2 8.3 %all_gather.11 = f32[512,128]{1,0:T(8,128)S(1)} all-gather(f32[64,128]{1,0:T(8,128)S(1)} %copy.25), channel_id=1, replica_groups=mesh['row'=8,'col'=4] {'row'}, dimensions={0}, use_global_device_ids=true | all-gather | bytes 294912 | tf_op jit(solution)/shard_map/all_gather | solution.py:42
  57.5 1.1 %convolution_bitcast_fusion = f32[64,512]{1,0:T(8,128)} fusion(f32[512,128]{1,0:T(8,128)S(1)} %all_gather.11, f32[64,128]{1,0:T(8,128)S(1)} %copy-done), kind=kOutput, calls=%fused_computation | convolution fusion | flops 50331648 | bytes 425984 | tf_op jit(solution)/shard_map/dot_general | solution.py:40
  58.7 0.8 negate_bitcast_fusion
  59.4 15.8 %reduce-scatter.6.cloned.1.call-done = f32[16,512]{1,0:T(8,128)} async-done(((f32[64,512]{1,0:T(8,128)}), f32[16,512]{1,0:T(8,128)}) %reduce-scatter.6.cloned.1.call-update) | async-done | bytes 32784 | tf_op jit(solution)/shard_map/reduce_scatter | solution.py:47
  75.3 1.4 %fusion.2 = f32[16,512]{1,0:T(8,128)S(1)} fusion(f32[16,512]{1,0:T(8,128)} %reduce-scatter.6.cloned.1.call-done, f32[2,512,512]{2,1,0:T(8,128)S(1)} %copy-done.1, f32[16,512]{1,0:T(8,128)} %reduce-scatter.4.cloned.1.call-done), kind=kOutput, calls=%fused_computation.10 | convolution fusion | flops 50356224 | bytes 1146880 | tf_op jit(solution)/shard_map/dot_general | solution.py:49
  76.6 18.5 %reduce-scatter.8.cloned.1.call-done = f32[16,512]{1,0:T(8,128)} async-done(((f32[64,512]{1,0:T(8,128)}), f32[16,512]{1,0:T(8,128)}) %reduce-scatter.8.cloned.1.call-update) | async-done | bytes 32784 | tf_op jit(solution)/shard_map/reduce_scatter | solution.py:47
  95.1 1.4 %fusion.1 = f32[1,16,512]{2,1,0:T(8,128)S(1)} fusion(f32[16,512]{1,0:T(8,128)} %reduce-scatter.8.cloned.1.call-done, f32[16,512]{1,0:T(8,128)S(1)} %fusion.2, f32[2,512,512]{2,1,0:T(8,128)S(1)} %copy-done.1), kind=kOutput, calls=%fused_computation.8 | convolution fusion | flops 50348032 | bytes 1146880 | tf_op jit(solution)/shard_map/dot_general | solution.py:49
  96.5 0.6 pad_maximum_fusion
  (34 shorter events, 2.7 us)
Async XLA Ops:
  6.5 30.0 %copy-start = (f32[64,128]{1,0:T(8,128)S(1)}, f32[64,128]{1,0:T(8,128)}, u32[]{:S(2)}) copy-start(f32[64,128]{1,0:T(8,128)} %param.6) | copy-start | bytes 98308
  6.5 52.1 %reduce-scatter.4.cloned.1.call-start = ((), (), s32[]{:S(2)}) async-start(), calls=%async_computation.3 | async-start | bytes 163840 | tf_op jit(solution)/shard_map/reduce_scatter | solution.py:47
  7.4 7.0 %collective-permute-start = (f32[64,64]{0,1:T(8,128)S(1)}, f32[64,64]{0,1:T(8,128)S(1)}, u32[]{:S(2)}, u32[]{:S(2)}) collective-permute-start(f32[64,64]{0,1:T(8,128)S(1)} %bitcast.65), channel_id=1, source_target_pairs={{0,1},{1,2},{2,3},{3,0},{4,5},{5,6},{6,7},{7,4},{8,9},{9,10},{10,1... | collective-permute-start | bytes 49160 | tf_op jit(solution)/shard_map/ppermute | solution.py:12
  10.6 6.1 %collective-permute-start.3 = (f32[64,64]{0,1:T(8,128)S(1)}, f32[64,64]{0,1:T(8,128)S(1)}, u32[]{:S(2)}, u32[]{:S(2)}) collective-permute-start(f32[64,64]{0,1:T(8,128)S(1)} %bitcast.61), channel_id=1, source_target_pairs={{0,1},{1,2},{2,3},{3,0},{4,5},{5,6},{6,7},{7,4},{8,9},{9,10},{10,1... | collective-permute-start | bytes 49160 | tf_op jit(solution)/shard_map/ppermute | solution.py:12
  12.2 5.9 %collective-permute-start.6 = (f32[64,64]{0,1:T(8,128)S(1)}, f32[64,64]{0,1:T(8,128)S(1)}, u32[]{:S(2)}, u32[]{:S(2)}) collective-permute-start(f32[64,64]{0,1:T(8,128)S(1)} %bitcast.63), channel_id=1, source_target_pairs={{0,1},{1,2},{2,3},{3,0},{4,5},{5,6},{6,7},{7,4},{8,9},{9,10},{10,1... | collective-permute-start | bytes 49160 | tf_op jit(solution)/shard_map/ppermute | solution.py:12
  14.4 5.7 %collective-permute-start.1 = (f32[64,64]{0,1:T(8,128)S(1)}, f32[64,64]{0,1:T(8,128)S(1)}, u32[]{:S(2)}, u32[]{:S(2)}) collective-permute-start(f32[64,64]{0,1:T(8,128)S(1)} %collective-permute-done), channel_id=1, source_target_pairs={{0,1},{1,2},{2,3},{3,0},{4,5},{5,6},{6,7},{7,4},{8,9},{9,10},{10,1... | collective-permute-start | bytes 49160 | tf_op jit(solution)/shard_map/ppermute | solution.py:12
  16.6 5.7 %collective-permute-start.4 = (f32[64,64]{0,1:T(8,128)S(1)}, f32[64,64]{0,1:T(8,128)S(1)}, u32[]{:S(2)}, u32[]{:S(2)}) collective-permute-start(f32[64,64]{0,1:T(8,128)S(1)} %collective-permute-done.3), channel_id=1, source_target_pairs={{0,1},{1,2},{2,3},{3,0},{4,5},{5,6},{6,7},{7,4},{8,9},{9,10},{10,1... | collective-permute-start | bytes 49160 | tf_op jit(solution)/shard_map/ppermute | solution.py:12
  18.2 5.9 %collective-permute-start.7 = (f32[64,64]{0,1:T(8,128)S(1)}, f32[64,64]{0,1:T(8,128)S(1)}, u32[]{:S(2)}, u32[]{:S(2)}) collective-permute-start(f32[64,64]{0,1:T(8,128)S(1)} %collective-permute-done.6), channel_id=1, source_target_pairs={{0,1},{1,2},{2,3},{3,0},{4,5},{5,6},{6,7},{7,4},{8,9},{9,10},{10,1... | collective-permute-start | bytes 49160 | tf_op jit(solution)/shard_map/ppermute | solution.py:12
  20.1 5.9 %collective-permute-start.2 = (f32[64,64]{0,1:T(8,128)S(1)}, f32[64,64]{0,1:T(8,128)S(1)}, u32[]{:S(2)}, u32[]{:S(2)}) collective-permute-start(f32[64,64]{0,1:T(8,128)S(1)} %collective-permute-done.1), channel_id=1, source_target_pairs={{0,1},{1,2},{2,3},{3,0},{4,5},{5,6},{6,7},{7,4},{8,9},{9,10},{10,1... | collective-permute-start | bytes 49160 | tf_op jit(solution)/shard_map/ppermute | solution.py:12
  22.4 15.3 %collective-permute-start.5 = (f32[64,64]{0,1:T(8,128)S(1)}, f32[64,64]{0,1:T(8,128)S(1)}, u32[]{:S(2)}, u32[]{:S(2)}) collective-permute-start(f32[64,64]{0,1:T(8,128)S(1)} %collective-permute-done.4), channel_id=1, source_target_pairs={{0,1},{1,2},{2,3},{3,0},{4,5},{5,6},{6,7},{7,4},{8,9},{9,10},{10,1... | collective-permute-start | bytes 49160 | tf_op jit(solution)/shard_map/ppermute | solution.py:12
  24.1 13.5 %collective-permute-start.8 = (f32[64,64]{0,1:T(8,128)S(1)}, f32[64,64]{0,1:T(8,128)S(1)}, u32[]{:S(2)}, u32[]{:S(2)}) collective-permute-start(f32[64,64]{0,1:T(8,128)S(1)} %collective-permute-done.7), channel_id=1, source_target_pairs={{0,1},{1,2},{2,3},{3,0},{4,5},{5,6},{6,7},{7,4},{8,9},{9,10},{10,1... | collective-permute-start | bytes 49160 | tf_op jit(solution)/shard_map/ppermute | solution.py:12
  26.6 48.7 %copy-start.1 = (f32[2,512,512]{2,1,0:T(8,128)S(1)}, f32[2,512,512]{2,1,0:T(8,128)}, u32[]{:S(2)}) copy-start(f32[2,512,512]{2,1,0:T(8,128)} %param.9) | copy-start | bytes 6291460
  37.6 37.6 %reduce-scatter.6.cloned.1.call-start = ((), (), s32[]{:S(2)}) async-start(), calls=%async_computation.4 | async-start | bytes 163840 | tf_op jit(solution)/shard_map/reduce_scatter | solution.py:47
  49.2 46.0 %reduce-scatter.8.cloned.1.call-start = ((), (), s32[]{:S(2)}) async-start(), calls=%async_computation.5 | async-start | bytes 163840 | tf_op jit(solution)/shard_map/reduce_scatter | solution.py:47
Sparse Core Ops, SparseCore 0:
  37.7 17.6 reduce-scatter.3
  57.7 17.5 reduce-scatter.5
  77.5 17.5 reduce-scatter.7
